TPU v7x, 32 devices: a whole 2x2x4 slice. The times are simulated.
32 devices in a mesh: cluster: 4 (over y, core), sub: 8 (over z, x).
Axes of the slice: x: 2, y: 2, z: 4, core: 2. Of those that a mesh axis runs over, the one named last changes fastest.
Arguments:
- load: float32 [57344, 256], P(('cluster', 'sub'))
- schur: float32 [57344, 1792], P(('cluster', 'sub')), as said below
- modes: float32 [57344, 128], P(('cluster', 'sub')), may hold values from -0.125 to 0.125
- coarse_inverse: float32 [4096, 1024], P(('cluster', 'sub')), as said below
- interface_rows: int32 [32], P(('cluster', 'sub')), may hold values from 896 to 1792, as said below
- mode_count: int32 [32], P(('cluster', 'sub')), may hold values from 64 to 128, as said below
- left_rows: int32 [32, 384], P(('cluster', 'sub')), may hold values from 0 to 1792, as said below
- right_rows: int32 [32, 384], P(('cluster', 'sub')), may hold values from 0 to 1792, as said below
Outputs:
- solution: float32 [57344, 256], P(('cluster', 'sub'))
- residual: float32 [57344, 256], P(('cluster', 'sub'))
Inputs may be any that keep to these rules, and one draw needn't show every extreme that they name: `interface_rows`: every subdomain has at least half of 1792 live rows, and some subdomain has exactly 1792. `mode_count`: every subdomain has at least half of 128 live modes, and some subdomain has exactly 128. Slot j of right_rows[g] and slot j of left_rows[g + 1] name the same interface unknown; the used slots of a row come first, all other slots hold 1792. Two neighbours share at least half of 384 rows and some pair shares exactly 384. The used entries of left_rows[g] and right_rows[g] are distinct live rows of g. left_rows[0] and right_rows[31] are unused. `right_rows`: see left_rows. `schur`: each block S_g is symmetric positive definite with a positive diagonal. `coarse_inverse`: each cluster's coarse inverse is symmetric positive definite.
All inputs are finite; a program needn't handle non-finite values.
Results may differ from a plain program's by a relative error of at most 0.0001.
Values sent between devices are 32-bit elements; how exact they have to be, the bound alone decides.
No kernel may reach another device: no remote copies, remote signals or barrier semaphores. Data moves between devices by JAX's collectives and lax.ppermute only.
A program may use at most 128 MiB of HBM per device.

v0:
```python
import jax
import jax.numpy as jnp
from jax import lax
from jax.sharding import PartitionSpec as P

ITERS = 3


def passed_along(value, axis, by):
    devices = lax.axis_size(axis)
    pairs = [(i, i + by) for i in range(devices) if 0 <= i + by < devices]
    return lax.ppermute(value, axis, pairs)


def take_rows(field, indices):
    return jnp.take(field, indices, axis=0, mode="fill", fill_value=0.0)


def assemble(field, left_index, right_index):
    to_left = take_rows(field, left_index)
    to_right = take_rows(field, right_index)
    from_left = passed_along(to_right, ("cluster", "sub"), 1)
    from_right = passed_along(to_left, ("cluster", "sub"), -1)
    merged = field.at[left_index].add(from_left, mode="drop")
    return merged.at[right_index].add(from_right, mode="drop")


def local(load, schur, modes, coarse_inverse, interface_rows, mode_count, left_rows, right_rows):
    highest = lax.Precision.HIGHEST
    order = schur.shape[0]
    mode_total = modes.shape[1]
    left_index = left_rows[0]
    right_index = right_rows[0]
    positions = jnp.arange(order, dtype=jnp.int32)
    live = (positions < interface_rows[0]).astype(jnp.float32)
    ones_shared = jnp.ones((left_index.shape[0],), jnp.float32)
    counted = jnp.zeros((order,), jnp.float32).at[left_index].add(ones_shared, mode="drop")
    counted = counted.at[right_index].add(ones_shared, mode="drop")
    share = (live / (1.0 + counted))[:, None]
    live_column = live[:, None]
    mode_live = (jnp.arange(mode_total, dtype=jnp.int32) < mode_count[0]).astype(jnp.float32)[
        :, None
    ]
    schur_diag = jnp.diagonal(schur)[:, None]
    rhs = assemble(live_column * load, left_index, right_index)
    solution = jnp.zeros_like(rhs)
    residual = rhs
    for iteration in range(ITERS):
        modal = jnp.einsum(
            "im,ik->mk",
            modes,
            share * residual,
            precision=highest,
            preferred_element_type=jnp.float32,
        )
        modal = modal * mode_live
        correction = jnp.dot(
            coarse_inverse,
            lax.all_gather(modal, "sub", axis=0, tiled=True),
            precision=highest,
            preferred_element_type=jnp.float32,
        )
        correction = correction * mode_live
        prolonged = jnp.dot(
            modes, correction, precision=highest, preferred_element_type=jnp.float32
        )
        direction = assemble(share * (prolonged + residual / schur_diag), left_index, right_index)
        product = jnp.dot(schur, direction, precision=highest, preferred_element_type=jnp.float32)
        image = assemble(live_column * product, left_index, right_index)
        numerator, denominator = lax.psum(
            (jnp.sum(share * residual * image, axis=0), jnp.sum(share * image * image, axis=0)),
            ("cluster", "sub"),
        )
        alpha = (numerator / (denominator + 1e-06))[None, :]
        solution = solution + alpha * direction
        residual = residual - alpha * image
    return (solution, residual)


def solution(mesh):
    return jax.shard_map(
        local,
        mesh=mesh,
        in_specs=(
            P(("cluster", "sub"), None),
            P(("cluster", "sub"), None),
            P(("cluster", "sub"), None),
            P(("cluster", "sub"), None),
            P(("cluster", "sub")),
            P(("cluster", "sub")),
            P(("cluster", "sub"), None),
            P(("cluster", "sub"), None),
        ),
        out_specs=(P(("cluster", "sub"), None), P(("cluster", "sub"), None)),
        check_vma=False,
    )
```

profile of v0, /device:TPU:10, one launch (start us, length us, event | category | flops | bytes accessed | tf_op | source)
XLA Modules:
  0.0 679.0 jit_solution(7623673633662888873)
XLA Ops:
  13.1 3.4 collective-permute-start
  22.2 3.5 scatter_custom_fusion
  26.4 3.6 scatter_fusion
  30.6 3.9 collective-permute-done
  34.5 5.1 scatter_fusion.1
  39.6 5.1 scatter_fusion.2
  49.5 28.0 %gather_fusion = f32[1792]{0:T(1024)S(1)} fusion(f32[1792,1792]{1,0:T(8,128)} %param.11, s32[1792]{0:T(1024)S(1)} %or_reduce_fusion), kind=kCustom, calls=%fused_computation.14 | custom fusion | bytes 28672 | tf_op jit(solution)/shard_map/jit(diagonal)/cond/branch_0_fun/gather | solution.py:44
  77.4 11.9 %all-gather.4.cloned.1.call-done = f32[1024,256]{0,1:T(8,128)} async-done(((f32[128,256]{0,1:T(8,128)}), f32[1024,256]{0,1:T(8,128)}) %all-gather.4.cloned.1.call-update) | async-done | bytes 1048592 | tf_op jit(solution)/shard_map/all_gather | solution.py:59
  91.5 4.4 add_multiply_fusion.2
  107.6 3.5 collective-permute-start.3
  111.1 11.5 %collective-permute-done.2 = f32[384,256]{1,0:T(8,128)} collective-permute-done((f32[384,256]{1,0:T(8,128)S(1)}, f32[384,256]{1,0:T(8,128)}, u32[]{:S(2)}, u32[]{:S(2)}) %collective-permute-start.2) | collective-permute-done | bytes 393248 | tf_op jit(solution)/shard_map/ppermute | solution.py:12
  122.6 3.8 scatter_fusion.3
  126.4 3.9 scatter_fusion.4
  130.3 27.1 %fusion = f32[1792,256]{0,1:T(8,128)} fusion(f32[1792,256]{1,0:T(8,128)S(1)} %scatter_fusion.4, f32[1792,1792]{1,0:T(8,128)} %param.11, f32[1792]{0:T(1024)S(1)} %fusion.33), kind=kOutput, calls=%fused_computation.40 | convolution fusion | flops 9865461760 | bytes 16522240 | tf_op jit(solution)/shard_map/dot_general | solution.py:68
  160.1 4.1 gather_fusion.6
  164.2 3.7 gather_fusion.5
  172.8 3.9 collective-permute-start.5
  176.7 10.5 %collective-permute-done.4 = f32[384,256]{1,0:T(8,128)} collective-permute-done((f32[384,256]{1,0:T(8,128)S(1)}, f32[384,256]{1,0:T(8,128)}, u32[]{:S(2)}, u32[]{:S(2)}) %collective-permute-start.4) | collective-permute-done | bytes 393248 | tf_op jit(solution)/shard_map/ppermute | solution.py:12
  187.2 5.6 scatter_fusion.5
  192.8 5.6 scatter_fusion.6
  203.6 43.9 %all-reduce.2 = (f32[256]{0:T(256)S(1)}, f32[256]{0:T(256)S(1)}) all-reduce(f32[256]{0:T(256)S(1)} %get-tuple-element.12, f32[256]{0:T(256)S(1)} %get-tuple-element.11), channel_id=1, replica_groups=mesh['cluster'=4,'sub'=8] {'cluster','sub'}, use_global_device_ids=true, to_apply=%region_9.11 | all-reduce | flops 512 | bytes 4096 | tf_op jit(solution)/shard_map/psum | solution.py:70
  253.4 37.5 %all-gather.6.cloned.1.call-done = f32[1024,256]{0,1:T(8,128)} async-done(((f32[128,256]{0,1:T(8,128)}), f32[1024,256]{0,1:T(8,128)}) %all-gather.6.cloned.1.call-update) | async-done | bytes 1048592 | tf_op jit(solution)/shard_map/all_gather | solution.py:59
  293.1 4.4 add_multiply_fusion.1
  300.2 3.7 gather_fusion.8
  303.9 3.7 gather_fusion.7
  316.4 11.7 %collective-permute-done.6 = f32[384,256]{1,0:T(8,128)} collective-permute-done((f32[384,256]{1,0:T(8,128)S(1)}, f32[384,256]{1,0:T(8,128)}, u32[]{:S(2)}, u32[]{:S(2)}) %collective-permute-start.6) | collective-permute-done | bytes 393248 | tf_op jit(solution)/shard_map/ppermute | solution.py:12
  328.0 5.6 scatter_fusion.7
  333.6 5.6 scatter_fusion.8
  339.3 27.7 %fusion.1 = f32[1792,256]{0,1:T(8,128)} fusion(f32[1792,256]{1,0:T(8,128)} %scatter_fusion.8, f32[1792,1792]{1,0:T(8,128)} %param.11, f32[1792]{0:T(1024)S(1)} %fusion.33), kind=kOutput, calls=%fused_computation.41 | convolution fusion | flops 9865461760 | bytes 16522240 | tf_op jit(solution)/shard_map/dot_general | solution.py:68
  369.7 4.1 gather_fusion.10
  373.8 3.7 gather_fusion.9
  382.4 3.9 collective-permute-start.9
  386.3 10.5 %collective-permute-done.8 = f32[384,256]{1,0:T(8,128)} collective-permute-done((f32[384,256]{1,0:T(8,128)S(1)}, f32[384,256]{1,0:T(8,128)}, u32[]{:S(2)}, u32[]{:S(2)}) %collective-permute-start.8) | collective-permute-done | bytes 393248 | tf_op jit(solution)/shard_map/ppermute | solution.py:12
  396.8 5.6 scatter_fusion.9
  402.4 5.6 scatter_fusion.10
  413.2 43.9 %all-reduce.1 = (f32[256]{0:T(256)S(1)}, f32[256]{0:T(256)S(1)}) all-reduce(f32[256]{0:T(256)S(1)} %get-tuple-element.10, f32[256]{0:T(256)S(1)} %get-tuple-element.9), channel_id=1, replica_groups=mesh['cluster'=4,'sub'=8] {'cluster','sub'}, use_global_device_ids=true, to_apply=%region_17.19 | all-reduce | flops 512 | bytes 4096 | tf_op jit(solution)/shard_map/psum | solution.py:70
  462.9 37.5 %all-gather.8.cloned.1.call-done = f32[1024,256]{0,1:T(8,128)} async-done(((f32[128,256]{0,1:T(8,128)}), f32[1024,256]{0,1:T(8,128)}) %all-gather.8.cloned.1.call-update) | async-done | bytes 1048592 | tf_op jit(solution)/shard_map/all_gather | solution.py:59
  502.7 4.4 add_multiply_fusion
  524.4 11.9 %collective-permute-done.10 = f32[384,256]{1,0:T(8,128)S(1)} collective-permute-done((f32[384,256]{1,0:T(8,128)S(1)}, f32[384,256]{1,0:T(8,128)S(1)}, u32[]{:S(2)}, u32[]{:S(2)}) %collective-permute-start.10) | collective-permute-done | bytes 393248 | tf_op jit(solution)/shard_map/ppermute | solution.py:12
  536.3 5.3 scatter_fusion.11
  541.6 5.3 scatter_fusion.12
  547.0 27.7 %fusion.2 = f32[1792,256]{0,1:T(8,128)} fusion(f32[1792,256]{1,0:T(8,128)} %scatter_fusion.12, f32[1792,1792]{1,0:T(8,128)} %param.11, f32[1792]{0:T(1024)S(1)} %fusion.33), kind=kOutput, calls=%fused_computation.42 | convolution fusion | flops 9865461760 | bytes 16522240 | tf_op jit(solution)/shard_map/dot_general | solution.py:68
  588.3 3.9 collective-permute-start.13
  598.5 4.6 collective-permute-done.12
  603.2 5.1 scatter_fusion.13
  608.3 5.1 scatter_fusion.14
  618.2 43.9 %all-reduce = (f32[256]{0:T(256)S(1)}, f32[256]{0:T(256)S(1)}) all-reduce(f32[256]{0:T(256)S(1)} %get-tuple-element.8, f32[256]{0:T(256)S(1)} %get-tuple-element.7), channel_id=1, replica_groups=mesh['cluster'=4,'sub'=8] {'cluster','sub'}, use_global_device_ids=true, to_apply=%region_25.27 | all-reduce | flops 512 | bytes 4096 | tf_op jit(solution)/shard_map/psum | solution.py:70
  662.1 5.6 multiply_subtract_fusion
  (153 shorter events, 129.9 us)
Async XLA Ops:
  7.2 39.4 %copy-start = (f32[1792,128]{1,0:T(8,128)S(1)}, f32[1792,128]{1,0:T(8,128)}, u32[]{:S(2)}) copy-start(f32[1792,128]{1,0:T(8,128)} %param.12) | copy-start | bytes 2752516
  7.2 82.1 %all-gather.4.cloned.1.call-start = ((), (), s32[]{:S(2)}) async-start(), calls=%async_computation | async-start | bytes 1179648 | tf_op jit(solution)/shard_map/all_gather | solution.py:59
  8.0 4.2 copy-start.21
  8.7 1.8 copy-start.15
  10.5 6.1 copy-start.2
  10.5 6.0 copy-start.31
  13.1 21.4 %collective-permute-start = (f32[384,256]{1,0:T(8,128)}, f32[384,256]{1,0:T(8,128)S(1)}, u32[]{:S(2)}, u32[]{:S(2)}) collective-permute-start(f32[384,256]{1,0:T(8,128)} %broadcast_select_fusion.13), channel_id=1, source_target_pairs={{0,1},{1,2},{2,3},{3,4},{4,5},{5,6},{6,7},{7,8},{8,9},{9,10},{10,1... | collective-permute-start | bytes 1179656 | tf_op jit(solution)/shard_map/ppermute | solution.py:12
  16.6 1.9 copy-start.24
  16.6 1.8 copy-start.18
  18.5 21.1 %collective-permute-start.1 = (f32[384,256]{1,0:T(8,128)S(1)}, f32[384,256]{1,0:T(8,128)S(1)}, u32[]{:S(2)}, u32[]{:S(2)}) collective-permute-start(f32[384,256]{1,0:T(8,128)S(1)} %broadcast_select_fusion.12), channel_id=1, source_target_pairs={{1,0},{2,1},{3,2},{4,3},{5,4},{6,5},{7,6},{8,7},{9,8},{10,9},{11,1... | collective-permute-start | bytes 1179656 | tf_op jit(solution)/shard_map/ppermute | solution.py:12
  21.6 12.9 %copy-start.12 = (s32[384]{0:T(512)}, s32[384]{0:T(512)S(1)}, u32[]{:S(2)}) copy-start(s32[384]{0:T(512)S(1)} %fusion.37) | copy-start | bytes 4612
  26.4 13.2 %copy-start.9 = (s32[384]{0:T(512)}, s32[384]{0:T(512)S(1)}, u32[]{:S(2)}) copy-start(s32[384]{0:T(512)S(1)} %fusion.38) | copy-start | bytes 4612
  44.7 1.8 copy-start.26
  46.5 2.3 copy-start.3
  48.9 242.0 %all-gather.6.cloned.1.call-start = ((), (), s32[]{:S(2)}) async-start(), calls=%async_computation.1 | async-start | bytes 1179648 | tf_op jit(solution)/shard_map/all_gather | solution.py:59
  49.4 39.8 %copy-start.8 = (f32[128,1024]{1,0:T(8,128)S(1)}, f32[128,1024]{1,0:T(8,128)}, u32[]{:S(2)}) copy-start(f32[128,1024]{1,0:T(8,128)} %param.13) | copy-start | bytes 1572868
  95.9 1.8 copy-start.19
  97.7 2.2 copy-start.16
  99.9 2.2 copy-start.22
  99.9 5.8 copy-start.25
  99.9 22.7 %copy-start.13 = (s32[384]{0:T(512)S(1)}, s32[384]{0:T(512)}, u32[]{:S(2)}) copy-start(s32[384]{0:T(512)} %copy-done.12) | copy-start | bytes 4612
  103.2 19.4 %collective-permute-start.2 = (f32[384,256]{1,0:T(8,128)S(1)}, f32[384,256]{1,0:T(8,128)}, u32[]{:S(2)}, u32[]{:S(2)}) collective-permute-start(f32[384,256]{1,0:T(8,128)S(1)} %broadcast_select_fusion.11), channel_id=1, source_target_pairs={{0,1},{1,2},{2,3},{3,4},{4,5},{5,6},{6,7},{7,8},{8,9},{9,10},{10,1... | collective-permute-start | bytes 1179656 | tf_op jit(solution)/shard_map/ppermute | solution.py:12
  107.6 18.8 %copy-start.10 = (s32[384]{0:T(512)S(1)}, s32[384]{0:T(512)}, u32[]{:S(2)}) copy-start(s32[384]{0:T(512)} %copy-done.9) | copy-start | bytes 4612
  107.6 18.7 %collective-permute-start.3 = (f32[384,256]{1,0:T(8,128)}, f32[384,256]{1,0:T(8,128)}, u32[]{:S(2)}, u32[]{:S(2)}) collective-permute-start(f32[384,256]{1,0:T(8,128)} %broadcast_select_fusion.10), channel_id=1, source_target_pairs={{1,0},{2,1},{3,2},{4,3},{5,4},{6,5},{7,6},{8,7},{9,8},{10,9},{11,1... | collective-permute-start | bytes 1179656 | tf_op jit(solution)/shard_map/ppermute | solution.py:12
  169.0 18.2 %collective-permute-start.4 = (f32[384,256]{1,0:T(8,128)S(1)}, f32[384,256]{1,0:T(8,128)}, u32[]{:S(2)}, u32[]{:S(2)}) collective-permute-start(f32[384,256]{1,0:T(8,128)S(1)} %broadcast_select_fusion.9), channel_id=1, source_target_pairs={{0,1},{1,2},{2,3},{3,4},{4,5},{5,6},{6,7},{7,8},{8,9},{9,10},{10,1... | collective-permute-start | bytes 1179656 | tf_op jit(solution)/shard_map/ppermute | solution.py:12
  172.8 20.0 %collective-permute-start.5 = (f32[384,256]{1,0:T(8,128)}, f32[384,256]{1,0:T(8,128)}, u32[]{:S(2)}, u32[]{:S(2)}) collective-permute-start(f32[384,256]{1,0:T(8,128)} %broadcast_select_fusion.8), channel_id=1, source_target_pairs={{1,0},{2,1},{3,2},{4,3},{5,4},{6,5},{7,6},{8,7},{9,8},{10,9},{11,1... | collective-permute-start | bytes 1179656 | tf_op jit(solution)/shard_map/ppermute | solution.py:12
  247.5 2.3 copy-start.27
  253.3 247.1 %all-gather.8.cloned.1.call-start = ((), (), s32[]{:S(2)}) async-start(), calls=%async_computation.2 | async-start | bytes 1179648 | tf_op jit(solution)/shard_map/all_gather | solution.py:59
  308.7 19.4 %collective-permute-start.6 = (f32[384,256]{1,0:T(8,128)S(1)}, f32[384,256]{1,0:T(8,128)}, u32[]{:S(2)}, u32[]{:S(2)}) collective-permute-start(f32[384,256]{1,0:T(8,128)S(1)} %broadcast_select_fusion.7), channel_id=1, source_target_pairs={{0,1},{1,2},{2,3},{3,4},{4,5},{5,6},{6,7},{7,8},{8,9},{9,10},{10,1... | collective-permute-start | bytes 1179656 | tf_op jit(solution)/shard_map/ppermute | solution.py:12
  313.0 20.6 %collective-permute-start.7 = (f32[384,256]{1,0:T(8,128)}, f32[384,256]{1,0:T(8,128)}, u32[]{:S(2)}, u32[]{:S(2)}) collective-permute-start(f32[384,256]{1,0:T(8,128)} %broadcast_select_fusion.6), channel_id=1, source_target_pairs={{1,0},{2,1},{3,2},{4,3},{5,4},{6,5},{7,6},{8,7},{9,8},{10,9},{11,1... | collective-permute-start | bytes 1179656 | tf_op jit(solution)/shard_map/ppermute | solution.py:12
  378.6 18.2 %collective-permute-start.8 = (f32[384,256]{1,0:T(8,128)S(1)}, f32[384,256]{1,0:T(8,128)}, u32[]{:S(2)}, u32[]{:S(2)}) collective-permute-start(f32[384,256]{1,0:T(8,128)S(1)} %broadcast_select_fusion.5), channel_id=1, source_target_pairs={{0,1},{1,2},{2,3},{3,4},{4,5},{5,6},{6,7},{7,8},{8,9},{9,10},{10,1... | collective-permute-start | bytes 1179656 | tf_op jit(solution)/shard_map/ppermute | solution.py:12
  382.4 20.0 %collective-permute-start.9 = (f32[384,256]{1,0:T(8,128)}, f32[384,256]{1,0:T(8,128)}, u32[]{:S(2)}, u32[]{:S(2)}) collective-permute-start(f32[384,256]{1,0:T(8,128)} %broadcast_select_fusion.4), channel_id=1, source_target_pairs={{1,0},{2,1},{3,2},{4,3},{5,4},{6,5},{7,6},{8,7},{9,8},{10,9},{11,1... | collective-permute-start | bytes 1179656 | tf_op jit(solution)/shard_map/ppermute | solution.py:12
  457.1 2.3 copy-start.29
  459.4 1.2 copy-start.5
  517.0 19.3 %collective-permute-start.10 = (f32[384,256]{1,0:T(8,128)S(1)}, f32[384,256]{1,0:T(8,128)S(1)}, u32[]{:S(2)}, u32[]{:S(2)}) collective-permute-start(f32[384,256]{1,0:T(8,128)S(1)} %broadcast_select_fusion.3), channel_id=1, source_target_pairs={{0,1},{1,2},{2,3},{3,4},{4,5},{5,6},{6,7},{7,8},{8,9},{9,10},{10,1... | collective-permute-start | bytes 1179656 | tf_op jit(solution)/shard_map/ppermute | solution.py:12
  521.0 20.6 %collective-permute-start.11 = (f32[384,256]{1,0:T(8,128)}, f32[384,256]{1,0:T(8,128)S(1)}, u32[]{:S(2)}, u32[]{:S(2)}) collective-permute-start(f32[384,256]{1,0:T(8,128)} %broadcast_select_fusion.2), channel_id=1, source_target_pairs={{1,0},{2,1},{3,2},{4,3},{5,4},{6,5},{7,6},{8,7},{9,8},{10,9},{11,1... | collective-permute-start | bytes 1179656 | tf_op jit(solution)/shard_map/ppermute | solution.py:12
  574.7 2.7 copy-start.20
  577.4 3.4 copy-start.17
  580.8 3.2 copy-start.23
  584.9 18.3 %collective-permute-start.12 = (f32[384,256]{1,0:T(8,128)}, f32[384,256]{1,0:T(8,128)S(1)}, u32[]{:S(2)}, u32[]{:S(2)}) collective-permute-start(f32[384,256]{1,0:T(8,128)} %broadcast_select_fusion.1), channel_id=1, source_target_pairs={{0,1},{1,2},{2,3},{3,4},{4,5},{5,6},{6,7},{7,8},{8,9},{9,10},{10,1... | collective-permute-start | bytes 1179656 | tf_op jit(solution)/shard_map/ppermute | solution.py:12
  588.3 20.0 %collective-permute-start.13 = (f32[384,256]{1,0:T(8,128)}, f32[384,256]{1,0:T(8,128)S(1)}, u32[]{:S(2)}, u32[]{:S(2)}) collective-permute-start(f32[384,256]{1,0:T(8,128)} %broadcast_select_fusion), channel_id=1, source_target_pairs={{1,0},{2,1},{3,2},{4,3},{5,4},{6,5},{7,6},{8,7},{9,8},{10,9},{11,1... | collective-permute-start | bytes 1179656 | tf_op jit(solution)/shard_map/ppermute | solution.py:12
  593.9 2.9 copy-start.1
  596.8 6.4 copy-start.14
  598.5 9.8 %copy-start.11 = (s32[384]{0:T(512)S(1)}, s32[384]{0:T(512)}, u32[]{:S(2)}) copy-start(s32[384]{0:T(512)} %copy-done.9) | copy-start | bytes 4612
  613.4 2.9 copy-start.6
  616.3 45.8 %copy-start.28 = (f32[256]{0:T(256)S(1)}, f32[256]{0:T(256)}, u32[]{:S(2)}) copy-start(f32[256]{0:T(256)} %copy-done.27) | copy-start | bytes 3076
  616.3 45.8 %copy-start.30 = (f32[256]{0:T(256)S(1)}, f32[256]{0:T(256)}, u32[]{:S(2)}) copy-start(f32[256]{0:T(256)} %copy-done.29) | copy-start | bytes 3076
  667.7 2.9 copy-start.7
  (1 other events, 1.2 us)
Sparse Core Ops, SparseCore 0:
  49.0 40.2 all-gather.3
  253.4 37.3 all-gather.5
  463.0 37.3 all-gather.7
where the time goes:
time: 690 us; the launch traced here: 679 us
  waiting for transfers between devices  152 us (22%)
  blocking collectives  132 us (19%)
  other arithmetic  119 us (17%)
  local copies, waits for them, and re-layouts  111 us (16%)
  matrix products  109 us (16%)
  starting transfers between devices  41.1 us (6%)
  between operations  15.9 us (2%)
    psum x3, blocking collectives, local(): lax.psum((jnp.sum(share * residual * image, axis=0), jnp.sum(share * imag...  132 us
    all_gather x3, waiting for transfers between devices, local(): lax.all_gather(modal, 'sub', axis=0, tiled=True)  86.9 us
    dot_general x3, matrix products, local(): jnp.dot(schur, direction, precision=highest, preferred_element_type=jnp.f...  82.5 us
    ppermute x14, waiting for transfers between devices, passed_along(): return lax.ppermute(value, axis, pairs)  64.6 us
    gather x14, local copies, waits for them, and re-layouts, take_rows(): return jnp.take(field, indices, axis=0, mode='fill', fill_value=0.0)  43.5 us
    ppermute x14, starting transfers between devices, passed_along(): return lax.ppermute(value, axis, pairs)  40.9 us
    scatter-add x7, other arithmetic, assemble(): return merged.at[right_index].add(from_right, mode='drop')  36.3 us
    scatter-add x7, other arithmetic, assemble(): merged = field.at[left_index].add(from_left, mode='drop')  36.1 us
  transfers between devices with their start and end apart: 17, of which 10 were waited for; matrix products, arithmetic and copies ran while one was open for 14% of the time, Pallas kernels for 0%

commit v1 on v0

--- a/solution.py
+++ b/solution.py
@@ -56,7 +56,9 @@
         modal = modal * mode_live
         correction = jnp.dot(
             coarse_inverse,
-            lax.all_gather(modal, "sub", axis=0, tiled=True),
+            jnp.concatenate(
+                lax.all_to_all(jnp.stack([modal] * lax.axis_size("sub")), "sub", 0, 0), axis=0
+            ),
             precision=highest,
             preferred_element_type=jnp.float32,
         )

time: 690 us -> 641 us (0.929)
  waiting for transfers between devices: 152 us -> 65.5 us
  blocking collectives: 132 us -> 181 us
  between operations: 15.9 us -> 3 us
    all_gather x3 -> x0, waiting for transfers between devices: 86.9 us -> none  [local(): lax.all_gather(modal, 'sub', axis=0, tiled=True)]
    all_to_all x0 -> x2, blocking collectives: none -> 54.7 us  [local(): lax.all_to_all(jnp.stack([modal] * lax.axis_size('sub')), 'sub', 0, 0)]
  transfers between devices with their start and end apart: 17 -> 15, of which waited for: 10 -> 7; matrix products, arithmetic and copies ran while one was open for 14% -> 15% of each run, Pallas kernels for 0% -> 0%
where the time goes in v1:
time: 641 us; the launch traced here: 630 us
  blocking collectives  181 us (28%)
  other arithmetic  119 us (19%)
  local copies, waits for them, and re-layouts  112 us (17%)
  matrix products  103 us (16%)
  waiting for transfers between devices  65.5 us (10%)
  starting transfers between devices  46.3 us (7%)
    psum x3, blocking collectives, local(): lax.psum((jnp.sum(share * residual * image, axis=0), jnp.sum(share * imag...  127 us
    dot_general x3, matrix products, local(): jnp.dot(schur, direction, precision=highest, preferred_element_type=jnp.f...  82.5 us
    ppermute x14, waiting for transfers between devices, passed_along(): return lax.ppermute(value, axis, pairs)  65.5 us
    all_to_all x2, blocking collectives, local(): lax.all_to_all(jnp.stack([modal] * lax.axis_size('sub')), 'sub', 0, 0)  54.7 us
    gather x14, local copies, waits for them, and re-layouts, take_rows(): return jnp.take(field, indices, axis=0, mode='fill', fill_value=0.0)  43.2 us
    ppermute x14, starting transfers between devices, passed_along(): return lax.ppermute(value, axis, pairs)  41.1 us
    scatter-add x7, other arithmetic, assemble(): return merged.at[right_index].add(from_right, mode='drop')  36.3 us
    scatter-add x7, other arithmetic, assemble(): merged = field.at[left_index].add(from_left, mode='drop')  36.1 us
  transfers between devices with their start and end apart: 15, of which 7 were waited for; matrix products, arithmetic and copies ran while one was open for 15% of the time, Pallas kernels for 0%

profile of v1, /device:TPU:10, one launch (start us, length us, event | category | flops | bytes accessed | tf_op | source)
XLA Modules:
  0.0 630.0 jit_solution(9794008122226122836)
XLA Ops:
  6.5 3.4 collective-permute-start
  15.7 3.5 scatter_custom_fusion
  19.9 3.6 scatter_fusion
  24.0 3.9 collective-permute-done
  27.9 5.1 scatter_fusion.1
  33.0 5.1 scatter_fusion.2
  42.8 5.2 all-to-all-start
  48.5 28.0 %gather_fusion = f32[1792]{0:T(1024)S(1)} fusion(f32[1792,1792]{1,0:T(8,128)} %param.11, s32[1792]{0:T(1024)S(1)} %or_reduce_fusion), kind=kCustom, calls=%fused_computation.14 | custom fusion | bytes 28672 | tf_op jit(solution)/shard_map/jit(diagonal)/cond/branch_0_fun/gather | solution.py:44
  78.3 4.4 add_multiply_fusion.2
  90.0 3.4 collective-permute-start.2
  97.9 12.0 %collective-permute-done.2 = f32[384,256]{1,0:T(8,128)} collective-permute-done((f32[384,256]{1,0:T(8,128)S(1)}, f32[384,256]{1,0:T(8,128)}, u32[]{:S(2)}, u32[]{:S(2)}) %collective-permute-start.2) | collective-permute-done | bytes 393248 | tf_op jit(solution)/shard_map/ppermute | solution.py:12
  109.9 3.8 scatter_fusion.3
  113.7 3.9 scatter_fusion.4
  117.7 27.1 %fusion = f32[1792,256]{0,1:T(8,128)} fusion(f32[1792,256]{1,0:T(8,128)S(1)} %scatter_fusion.4, f32[1792,1792]{1,0:T(8,128)} %param.11, f32[1792]{0:T(1024)S(1)} %fusion.33), kind=kOutput, calls=%fused_computation.40 | convolution fusion | flops 9865461760 | bytes 16522240 | tf_op jit(solution)/shard_map/dot_general | solution.py:70
  147.5 3.9 gather_fusion.6
  151.3 3.7 gather_fusion.5
  160.3 3.6 collective-permute-start.5
  163.9 10.5 %collective-permute-done.4 = f32[384,256]{1,0:T(8,128)} collective-permute-done((f32[384,256]{1,0:T(8,128)S(1)}, f32[384,256]{1,0:T(8,128)}, u32[]{:S(2)}, u32[]{:S(2)}) %collective-permute-start.4) | collective-permute-done | bytes 393248 | tf_op jit(solution)/shard_map/ppermute | solution.py:12
  174.3 5.6 scatter_fusion.5
  179.9 5.6 scatter_fusion.6
  190.7 41.5 %all-reduce.2 = (f32[256]{0:T(256)S(1)}, f32[256]{0:T(256)S(1)}) all-reduce(f32[256]{0:T(256)S(1)} %get-tuple-element.12, f32[256]{0:T(256)S(1)} %get-tuple-element.11), channel_id=1, replica_groups=mesh['cluster'=4,'sub'=8] {'cluster','sub'}, use_global_device_ids=true, to_apply=%region_9.11 | all-reduce | flops 512 | bytes 4096 | tf_op jit(solution)/shard_map/psum | solution.py:72
  237.7 27.9 %all_to_all.15 = f32[8,128,256]{2,1,0:T(8,128)S(1)} all-to-all(f32[8,128,256]{2,1,0:T(8,128)S(1)} %stack.7), channel_id=1, replica_groups=mesh['cluster'=4,'sub'=8] {'sub'}, dimensions={0} | all-to-all | bytes 2097152 | tf_op jit(solution)/shard_map/all_to_all | solution.py:60
  273.1 3.7 gather_fusion.8
  276.8 3.7 gather_fusion.7
  281.6 3.7 collective-permute-start.6
  289.4 11.8 %collective-permute-done.6 = f32[384,256]{1,0:T(8,128)} collective-permute-done((f32[384,256]{1,0:T(8,128)S(1)}, f32[384,256]{1,0:T(8,128)}, u32[]{:S(2)}, u32[]{:S(2)}) %collective-permute-start.6) | collective-permute-done | bytes 393248 | tf_op jit(solution)/shard_map/ppermute | solution.py:12
  301.3 5.6 scatter_fusion.7
  306.9 5.6 scatter_fusion.8
  312.5 27.7 %fusion.1 = f32[1792,256]{0,1:T(8,128)} fusion(f32[1792,256]{1,0:T(8,128)} %scatter_fusion.8, f32[1792,1792]{1,0:T(8,128)} %param.11, f32[1792]{0:T(1024)S(1)} %fusion.33), kind=kOutput, calls=%fused_computation.41 | convolution fusion | flops 9865461760 | bytes 16522240 | tf_op jit(solution)/shard_map/dot_general | solution.py:70
  343.0 3.9 gather_fusion.10
  346.9 3.7 gather_fusion.9
  355.4 3.9 collective-permute-start.9
  359.4 10.5 %collective-permute-done.8 = f32[384,256]{1,0:T(8,128)} collective-permute-done((f32[384,256]{1,0:T(8,128)S(1)}, f32[384,256]{1,0:T(8,128)}, u32[]{:S(2)}, u32[]{:S(2)}) %collective-permute-start.8) | collective-permute-done | bytes 393248 | tf_op jit(solution)/shard_map/ppermute | solution.py:12
  369.9 5.6 scatter_fusion.9
  375.4 5.6 scatter_fusion.10
  386.2 42.5 %all-reduce.1 = (f32[256]{0:T(256)S(1)}, f32[256]{0:T(256)S(1)}) all-reduce(f32[256]{0:T(256)S(1)} %get-tuple-element.10, f32[256]{0:T(256)S(1)} %get-tuple-element.9), channel_id=1, replica_groups=mesh['cluster'=4,'sub'=8] {'cluster','sub'}, use_global_device_ids=true, to_apply=%region_17.19 | all-reduce | flops 512 | bytes 4096 | tf_op jit(solution)/shard_map/psum | solution.py:72
  434.2 26.7 %all_to_all.16 = f32[8,128,256]{2,1,0:T(8,128)S(1)} all-to-all(f32[8,128,256]{2,1,0:T(8,128)S(1)} %stack.8), channel_id=1, replica_groups=mesh['cluster'=4,'sub'=8] {'sub'}, dimensions={0} | all-to-all | bytes 2097152 | tf_op jit(solution)/shard_map/all_to_all | solution.py:60
  475.6 3.7 collective-permute-start.10
  483.0 12.2 %collective-permute-done.10 = f32[384,256]{1,0:T(8,128)S(1)} collective-permute-done((f32[384,256]{1,0:T(8,128)S(1)}, f32[384,256]{1,0:T(8,128)S(1)}, u32[]{:S(2)}, u32[]{:S(2)}) %collective-permute-start.10) | collective-permute-done | bytes 393248 | tf_op jit(solution)/shard_map/ppermute | solution.py:12
  495.2 5.3 scatter_fusion.11
  500.5 5.3 scatter_fusion.12
  505.9 27.7 %fusion.2 = f32[1792,256]{0,1:T(8,128)} fusion(f32[1792,256]{1,0:T(8,128)} %scatter_fusion.12, f32[1792,1792]{1,0:T(8,128)} %param.11, f32[1792]{0:T(1024)S(1)} %fusion.33), kind=kOutput, calls=%fused_computation.42 | convolution fusion | flops 9865461760 | bytes 16522240 | tf_op jit(solution)/shard_map/dot_general | solution.py:70
  547.2 3.9 collective-permute-start.13
  557.5 4.6 collective-permute-done.12
  562.0 5.1 scatter_fusion.13
  567.2 5.1 scatter_fusion.14
  577.1 42.5 %all-reduce = (f32[256]{0:T(256)S(1)}, f32[256]{0:T(256)S(1)}) all-reduce(f32[256]{0:T(256)S(1)} %get-tuple-element.8, f32[256]{0:T(256)S(1)} %get-tuple-element.7), channel_id=1, replica_groups=mesh['cluster'=4,'sub'=8] {'cluster','sub'}, use_global_device_ids=true, to_apply=%region_25.27 | all-reduce | flops 512 | bytes 4096 | tf_op jit(solution)/shard_map/psum | solution.py:72
  619.7 5.6 multiply_subtract_fusion
  (186 shorter events, 127.2 us)
Async XLA Ops:
  0.6 39.3 %copy-start = (f32[1792,128]{1,0:T(8,128)S(1)}, f32[1792,128]{1,0:T(8,128)}, u32[]{:S(2)}) copy-start(f32[1792,128]{1,0:T(8,128)} %param.12) | copy-start | bytes 2752516
  1.4 4.2 copy-start.28
  4.0 6.1 copy-start.2
  4.0 6.0 copy-start.47
  6.5 21.4 %collective-permute-start = (f32[384,256]{1,0:T(8,128)}, f32[384,256]{1,0:T(8,128)S(1)}, u32[]{:S(2)}, u32[]{:S(2)}) collective-permute-start(f32[384,256]{1,0:T(8,128)} %broadcast_select_fusion.13), channel_id=1, source_target_pairs={{0,1},{1,2},{2,3},{3,4},{4,5},{5,6},{6,7},{7,8},{8,9},{9,10},{10,1... | collective-permute-start | bytes 1179656 | tf_op jit(solution)/shard_map/ppermute | solution.py:12
  11.9 21.1 %collective-permute-start.1 = (f32[384,256]{1,0:T(8,128)S(1)}, f32[384,256]{1,0:T(8,128)S(1)}, u32[]{:S(2)}, u32[]{:S(2)}) collective-permute-start(f32[384,256]{1,0:T(8,128)S(1)} %broadcast_select_fusion.12), channel_id=1, source_target_pairs={{1,0},{2,1},{3,2},{4,3},{5,4},{6,5},{7,6},{8,7},{9,8},{10,9},{11,1... | collective-permute-start | bytes 1179656 | tf_op jit(solution)/shard_map/ppermute | solution.py:12
  15.0 12.9 %copy-start.15 = (s32[384]{0:T(512)}, s32[384]{0:T(512)S(1)}, u32[]{:S(2)}) copy-start(s32[384]{0:T(512)S(1)} %fusion.37) | copy-start | bytes 4612
  19.9 13.2 %copy-start.11 = (s32[384]{0:T(512)}, s32[384]{0:T(512)S(1)}, u32[]{:S(2)}) copy-start(s32[384]{0:T(512)S(1)} %fusion.38) | copy-start | bytes 4612
  42.8 33.7 %all-to-all-start = ((f32[8,128,256]{2,1,0:T(8,128)}), f32[8,128,256]{2,1,0:T(8,128)S(1)}, u32[]{:S(2)}, u32[]{:S(2)}) async-start(f32[8,128,256]{2,1,0:T(8,128)} %stack.6), calls=%async_computation | async-start | bytes 2097152 | tf_op jit(solution)/shard_map/all_to_all | solution.py:60
  48.5 28.0 %copy-start.10 = (f32[128,1024]{1,0:T(8,128)S(1)}, f32[128,1024]{1,0:T(8,128)}, u32[]{:S(2)}) copy-start(f32[128,1024]{1,0:T(8,128)} %param.13) | copy-start | bytes 1572868
  76.5 6.2 copy-start.44
  86.7 6.7 %copy-start.33 = (pred[384]{0:T(512)(128)(4,1)S(1)}, pred[384]{0:T(512)(128)(4,1)}, u32[]{:S(2)}) copy-start(pred[384]{0:T(512)(128)(4,1)} %copy-done.32) | copy-start | bytes 1156
  86.7 23.2 %copy-start.16 = (s32[384]{0:T(512)S(1)}, s32[384]{0:T(512)}, u32[]{:S(2)}) copy-start(s32[384]{0:T(512)} %copy-done.15) | copy-start | bytes 4612
  90.0 19.9 %collective-permute-start.2 = (f32[384,256]{1,0:T(8,128)S(1)}, f32[384,256]{1,0:T(8,128)}, u32[]{:S(2)}, u32[]{:S(2)}) collective-permute-start(f32[384,256]{1,0:T(8,128)S(1)} %broadcast_select_fusion.11), channel_id=1, source_target_pairs={{0,1},{1,2},{2,3},{3,4},{4,5},{5,6},{6,7},{7,8},{8,9},{9,10},{10,1... | collective-permute-start | bytes 1179656 | tf_op jit(solution)/shard_map/ppermute | solution.py:12
  95.3 18.4 %copy-start.12 = (s32[384]{0:T(512)S(1)}, s32[384]{0:T(512)}, u32[]{:S(2)}) copy-start(s32[384]{0:T(512)} %copy-done.11) | copy-start | bytes 4612
  95.3 18.4 %collective-permute-start.3 = (f32[384,256]{1,0:T(8,128)}, f32[384,256]{1,0:T(8,128)}, u32[]{:S(2)}, u32[]{:S(2)}) collective-permute-start(f32[384,256]{1,0:T(8,128)} %broadcast_select_fusion.10), channel_id=1, source_target_pairs={{1,0},{2,1},{3,2},{4,3},{5,4},{6,5},{7,6},{8,7},{9,8},{10,9},{11,1... | collective-permute-start | bytes 1179656 | tf_op jit(solution)/shard_map/ppermute | solution.py:12
  156.1 18.2 %collective-permute-start.4 = (f32[384,256]{1,0:T(8,128)S(1)}, f32[384,256]{1,0:T(8,128)}, u32[]{:S(2)}, u32[]{:S(2)}) collective-permute-start(f32[384,256]{1,0:T(8,128)S(1)} %broadcast_select_fusion.9), channel_id=1, source_target_pairs={{0,1},{1,2},{2,3},{3,4},{4,5},{5,6},{6,7},{7,8},{8,9},{9,10},{10,1... | collective-permute-start | bytes 1179656 | tf_op jit(solution)/shard_map/ppermute | solution.py:12
  160.3 19.7 %collective-permute-start.5 = (f32[384,256]{1,0:T(8,128)}, f32[384,256]{1,0:T(8,128)}, u32[]{:S(2)}, u32[]{:S(2)}) collective-permute-start(f32[384,256]{1,0:T(8,128)} %broadcast_select_fusion.8), channel_id=1, source_target_pairs={{1,0},{2,1},{3,2},{4,3},{5,4},{6,5},{7,6},{8,7},{9,8},{10,9},{11,1... | collective-permute-start | bytes 1179656 | tf_op jit(solution)/shard_map/ppermute | solution.py:12
  232.2 3.5 copy-start.36
  237.5 28.1 %copy-start.37 = (f32[128]{0:T(128)S(1)}, f32[128]{0:T(128)}, u32[]{:S(2)}) copy-start(f32[128]{0:T(128)} %compare_convert_fusion) | copy-start | bytes 1540
  237.6 29.8 %copy-start.5 = (f32[1792,256]{0,1:T(8,128)S(1)}, f32[1792,256]{0,1:T(8,128)}, u32[]{:S(2)}) copy-start(f32[1792,256]{0,1:T(8,128)} %copy-done.4) | copy-start | bytes 5505028
  237.7 29.8 %copy-start.45 = (f32[1792]{0:T(1024)S(1)}, f32[1792]{0:T(1024)}, u32[]{:S(2)}) copy-start(f32[1792]{0:T(1024)} %copy-done.44) | copy-start | bytes 21508
  273.1 3.7 copy-start.21
  276.8 3.7 copy-start.30
  276.8 8.5 %copy-start.34 = (pred[384]{0:T(512)(128)(4,1)S(1)}, pred[384]{0:T(512)(128)(4,1)}, u32[]{:S(2)}) copy-start(pred[384]{0:T(512)(128)(4,1)} %copy-done.32) | copy-start | bytes 1156
  276.8 24.5 %copy-start.17 = (s32[384]{0:T(512)S(1)}, s32[384]{0:T(512)}, u32[]{:S(2)}) copy-start(s32[384]{0:T(512)} %copy-done.15) | copy-start | bytes 4612
  281.6 19.7 %collective-permute-start.6 = (f32[384,256]{1,0:T(8,128)S(1)}, f32[384,256]{1,0:T(8,128)}, u32[]{:S(2)}, u32[]{:S(2)}) collective-permute-start(f32[384,256]{1,0:T(8,128)S(1)} %broadcast_select_fusion.7), channel_id=1, source_target_pairs={{0,1},{1,2},{2,3},{3,4},{4,5},{5,6},{6,7},{7,8},{8,9},{9,10},{10,1... | collective-permute-start | bytes 1179656 | tf_op jit(solution)/shard_map/ppermute | solution.py:12
  287.1 19.7 %copy-start.13 = (s32[384]{0:T(512)S(1)}, s32[384]{0:T(512)}, u32[]{:S(2)}) copy-start(s32[384]{0:T(512)} %copy-done.11) | copy-start | bytes 4612
  287.1 19.7 %collective-permute-start.7 = (f32[384,256]{1,0:T(8,128)}, f32[384,256]{1,0:T(8,128)}, u32[]{:S(2)}, u32[]{:S(2)}) collective-permute-start(f32[384,256]{1,0:T(8,128)} %broadcast_select_fusion.6), channel_id=1, source_target_pairs={{1,0},{2,1},{3,2},{4,3},{5,4},{6,5},{7,6},{8,7},{9,8},{10,9},{11,1... | collective-permute-start | bytes 1179656 | tf_op jit(solution)/shard_map/ppermute | solution.py:12
  351.7 18.2 %collective-permute-start.8 = (f32[384,256]{1,0:T(8,128)S(1)}, f32[384,256]{1,0:T(8,128)}, u32[]{:S(2)}, u32[]{:S(2)}) collective-permute-start(f32[384,256]{1,0:T(8,128)S(1)} %broadcast_select_fusion.5), channel_id=1, source_target_pairs={{0,1},{1,2},{2,3},{3,4},{4,5},{5,6},{6,7},{7,8},{8,9},{9,10},{10,1... | collective-permute-start | bytes 1179656 | tf_op jit(solution)/shard_map/ppermute | solution.py:12
  355.4 20.0 %collective-permute-start.9 = (f32[384,256]{1,0:T(8,128)}, f32[384,256]{1,0:T(8,128)}, u32[]{:S(2)}, u32[]{:S(2)}) collective-permute-start(f32[384,256]{1,0:T(8,128)} %broadcast_select_fusion.4), channel_id=1, source_target_pairs={{1,0},{2,1},{3,2},{4,3},{5,4},{6,5},{7,6},{8,7},{9,8},{10,9},{11,1... | collective-permute-start | bytes 1179656 | tf_op jit(solution)/shard_map/ppermute | solution.py:12
  428.7 3.5 copy-start.38
  434.0 26.8 %copy-start.39 = (f32[128]{0:T(128)S(1)}, f32[128]{0:T(128)}, u32[]{:S(2)}) copy-start(f32[128]{0:T(128)} %compare_convert_fusion) | copy-start | bytes 1540
  434.1 28.5 %copy-start.7 = (f32[1792,256]{0,1:T(8,128)S(1)}, f32[1792,256]{0,1:T(8,128)}, u32[]{:S(2)}) copy-start(f32[1792,256]{0,1:T(8,128)} %copy-done.6) | copy-start | bytes 5505028
  434.2 28.5 %copy-start.46 = (f32[1792]{0:T(1024)S(1)}, f32[1792]{0:T(1024)}, u32[]{:S(2)}) copy-start(f32[1792]{0:T(1024)} %copy-done.44) | copy-start | bytes 21508
  475.6 19.6 %collective-permute-start.10 = (f32[384,256]{1,0:T(8,128)S(1)}, f32[384,256]{1,0:T(8,128)S(1)}, u32[]{:S(2)}, u32[]{:S(2)}) collective-permute-start(f32[384,256]{1,0:T(8,128)S(1)} %broadcast_select_fusion.3), channel_id=1, source_target_pairs={{0,1},{1,2},{2,3},{3,4},{4,5},{5,6},{6,7},{7,8},{8,9},{9,10},{10,1... | collective-permute-start | bytes 1179656 | tf_op jit(solution)/shard_map/ppermute | solution.py:12
  480.8 19.7 %collective-permute-start.11 = (f32[384,256]{1,0:T(8,128)}, f32[384,256]{1,0:T(8,128)S(1)}, u32[]{:S(2)}, u32[]{:S(2)}) collective-permute-start(f32[384,256]{1,0:T(8,128)} %broadcast_select_fusion.2), channel_id=1, source_target_pairs={{1,0},{2,1},{3,2},{4,3},{5,4},{6,5},{7,6},{8,7},{9,8},{10,9},{11,1... | collective-permute-start | bytes 1179656 | tf_op jit(solution)/shard_map/ppermute | solution.py:12
  536.3 3.4 copy-start.22
  539.7 3.2 copy-start.31
  543.7 18.3 %collective-permute-start.12 = (f32[384,256]{1,0:T(8,128)}, f32[384,256]{1,0:T(8,128)S(1)}, u32[]{:S(2)}, u32[]{:S(2)}) collective-permute-start(f32[384,256]{1,0:T(8,128)} %broadcast_select_fusion.1), channel_id=1, source_target_pairs={{0,1},{1,2},{2,3},{3,4},{4,5},{5,6},{6,7},{7,8},{8,9},{9,10},{10,1... | collective-permute-start | bytes 1179656 | tf_op jit(solution)/shard_map/ppermute | solution.py:12
  547.2 20.0 %collective-permute-start.13 = (f32[384,256]{1,0:T(8,128)}, f32[384,256]{1,0:T(8,128)S(1)}, u32[]{:S(2)}, u32[]{:S(2)}) collective-permute-start(f32[384,256]{1,0:T(8,128)} %broadcast_select_fusion), channel_id=1, source_target_pairs={{1,0},{2,1},{3,2},{4,3},{5,4},{6,5},{7,6},{8,7},{9,8},{10,9},{11,1... | collective-permute-start | bytes 1179656 | tf_op jit(solution)/shard_map/ppermute | solution.py:12
  552.8 2.9 copy-start.1
  555.8 6.3 copy-start.18
  557.5 9.7 %copy-start.14 = (s32[384]{0:T(512)S(1)}, s32[384]{0:T(512)}, u32[]{:S(2)}) copy-start(s32[384]{0:T(512)} %copy-done.11) | copy-start | bytes 4612
  572.3 2.9 copy-start.8
  575.2 44.5 %copy-start.41 = (f32[256]{0:T(256)S(1)}, f32[256]{0:T(256)}, u32[]{:S(2)}) copy-start(f32[256]{0:T(256)} %copy-done.40) | copy-start | bytes 3076
  575.2 44.5 %copy-start.43 = (f32[256]{0:T(256)S(1)}, f32[256]{0:T(256)}, u32[]{:S(2)}) copy-start(f32[256]{0:T(256)} %copy-done.42) | copy-start | bytes 3076
  625.3 2.9 copy-start.9
  (15 other events, 31.8 us)
